TPU v7x, 32 devices: a whole 2x2x4 slice. The times are simulated.
32 devices in a mesh: gen: 4 (over y, x), fit: 8 (over z, core).
Axes of the slice: x: 2, y: 2, z: 4, core: 2. Of those that a mesh axis runs over, the one named last changes fastest.
Arguments:
- raw_columns: bfloat16 [8, 2000, 2000], P(None, 'gen', 'fit'), as said below
- pivot_pairs: int32 [8], replicated, may hold values from 0 to 3999999, as said below
- collocation: bfloat16 [2000, 4096], P('gen', 'fit'), may hold values from -0.125 to 0.125
- metric_factor: float32 [4096, 4096], P('fit', 'gen'), as said below
Outputs:
- panel: float32 [8, 4096], P('gen', 'fit')
Inputs may be any that keep to these rules, and one draw needn't show every extreme that they name: `pivot_pairs`: 8 distinct orbital-pair indices p * 2000 + q. The entries at the pivots, raw_columns[P, pivot_pairs[Q] // 2000, pivot_pairs[Q] % 2000], form a symmetric positive definite matrix. `metric_factor`: lower triangular with a positive diagonal.
All inputs are finite; a program needn't handle non-finite values.
Results may differ from a plain program's by a relative error of at most 0.0029.
Values may be sent and summed in bfloat16 or wider, within the bound.
No kernel may reach another device: no remote copies, remote signals or barrier semaphores. Data moves between devices by JAX's collectives and lax.ppermute only.
A program may use at most 64 MiB of HBM per device.

v0:
```python
import math
import jax
import jax.numpy as jnp
from jax import lax
from jax.sharding import PartitionSpec as P

NORB = 2000


def spread(value, axis, source):
    kept = jnp.where(lax.axis_index(axis) == source, value, 0).astype(value.dtype)
    return lax.psum(kept, axis)


def project_block(vectors, stacked, orbital_count):
    point_count = stacked.shape[1]
    block_width = math.gcd(point_count, 512)
    block_count = point_count // block_width
    pair_count = stacked.shape[0] - orbital_count
    orbital_part = (
        stacked[:orbital_count].reshape(orbital_count, block_count, block_width).transpose(1, 0, 2)
    )
    pair_part = (
        stacked[orbital_count:].reshape(pair_count, block_count, block_width).transpose(1, 0, 2)
    )

    def one_block(pieces):
        mixed_terms = jnp.einsum(
            "apq,pn->aqn", vectors, pieces[0], preferred_element_type=jnp.float32
        )
        return jnp.sum(mixed_terms * pieces[1].astype(jnp.float32)[None], axis=1)

    blocks = lax.map(one_block, (orbital_part, pair_part))
    return blocks.transpose(1, 0, 2).reshape(vectors.shape[0], point_count)


def on_device(raw_columns, pivot_pairs, collocation, metric_factor):
    vec_total, orb_block, pair_block = raw_columns.shape
    gen_count = lax.axis_size("gen")
    fit_count = lax.axis_size("fit")
    gen_index = lax.axis_index("gen")
    fit_index = lax.axis_index("fit")
    point_dev = metric_factor.shape[0]
    vec_dev = vec_total // gen_count
    pair_first = pivot_pairs // NORB
    pair_second = pivot_pairs % NORB
    row_hits = (
        pair_first[:, None] == gen_index * orb_block + jnp.arange(orb_block)[None, :]
    ).astype(jnp.bfloat16)
    col_hits = (
        pair_second[:, None] == fit_index * pair_block + jnp.arange(pair_block)[None, :]
    ).astype(jnp.float32)
    picked = jnp.einsum("apq,bp->abq", raw_columns, row_hits, preferred_element_type=jnp.float32)
    own_entries = jnp.sum(picked * col_hits[None], axis=2)
    pivot_block = lax.psum(own_entries, ("gen", "fit"))
    factor = jnp.linalg.cholesky(pivot_block)
    flat_columns = raw_columns.reshape(vec_total, orb_block * pair_block).astype(jnp.float32)
    vectors = jax.scipy.linalg.solve_triangular(factor, flat_columns, lower=True)
    vectors = vectors.astype(jnp.bfloat16).reshape(vec_total, orb_block, pair_block)
    group_ratio = fit_count // gen_count
    owner_index = fit_index // group_ratio
    portion = fit_index % group_ratio
    orbital_side = lax.all_gather(collocation, "fit", axis=1, tiled=True)
    wide_slice = lax.dynamic_slice_in_dim(orbital_side, portion * pair_block, pair_block, 0)
    pair_side = spread(wide_slice, "gen", owner_index)
    partial_panel = project_block(
        vectors, jnp.concatenate([orbital_side, pair_side], axis=0), orb_block
    )
    arranged = partial_panel.reshape(gen_count, vec_dev, fit_count, point_dev).transpose(0, 2, 1, 3)
    arranged = arranged.reshape(gen_count * fit_count * vec_dev, point_dev)
    summed = lax.psum_scatter(arranged, ("gen", "fit"), scatter_dimension=0, tiled=True)
    remaining_start = jnp.zeros((vec_total, point_dev), jnp.float32)
    remaining_start = lax.dynamic_update_slice_in_dim(
        remaining_start, summed, gen_index * vec_dev, 0
    )

    def advance(turn_index, carried):
        remaining, solved = carried
        turn_owner = turn_index // group_ratio
        local_start = turn_index % group_ratio * point_dev
        whole_rest = lax.psum(remaining, "gen")
        column_part = lax.dynamic_slice_in_dim(metric_factor, local_start, point_dev, 1)
        candidate = jax.scipy.linalg.solve_triangular(column_part, whole_rest.T, lower=True).T
        holder = jnp.logical_and(fit_index == turn_index, gen_index == turn_owner)
        candidate = jnp.where(holder, candidate, 0.0)
        arrived = spread(candidate, ("gen", "fit"), turn_owner * fit_count + turn_index)
        update = jnp.dot(arrived, column_part.T, precision=lax.Precision.HIGHEST)
        remaining = remaining - jnp.where(gen_index == turn_owner, update, 0.0)
        own_rows = lax.dynamic_slice_in_dim(arrived, gen_index * vec_dev, vec_dev, 0)
        solved = jnp.where(fit_index == turn_index, own_rows, solved)
        return (remaining, solved)

    initial = jnp.zeros((vec_dev, point_dev), jnp.float32)
    remaining, solved = lax.fori_loop(0, fit_count, advance, (remaining_start, initial))
    return solved


def solution(mesh):
    in_specs = (P(None, "gen", "fit"), P(), P("gen", "fit"), P("fit", "gen"))
    out_specs = P("gen", "fit")
    return jax.shard_map(
        on_device, mesh=mesh, in_specs=in_specs, out_specs=out_specs, check_vma=False
    )
```

profile of v0, /device:TPU:0, one launch (start us, length us, event | category | flops | bytes accessed | tf_op | source)
XLA Modules:
  0.0 1175.4 jit_solution(14042528507513244858)
XLA Ops:
  7.3 50.9 %all-gather.2.cloned.1.call-done = bf16[500,4096]{1,0:T(8,128)(2,1)} async-done(((bf16[500,512]{1,0:T(8,128)(2,1)}), bf16[500,4096]{1,0:T(8,128)(2,1)}) %all-gather.2.cloned.1.call-update) | async-done | bytes 4096016 | tf_op jit(solution)/shard_map/all_gather | solution.py:63
  58.2 2.2 dynamic-slice_select_fusion
  60.4 2.5 copy.24
  67.0 39.1 %psum.42 = f32[8,8]{0,1:T(8,128)S(1)} all-reduce(f32[8,8]{0,1:T(8,128)S(1)} %bitcast.108), channel_id=1, replica_groups=mesh['gen'=4,'fit'=8] {'gen','fit'}, use_global_device_ids=true, to_apply=%region_2.3 | all-reduce | flops 64 | bytes 512 | tf_op jit(solution)/shard_map/psum | solution.py:55
  108.8 7.2 reshape.130
  116.0 4.1 reshape.104
  120.1 3.0 convolution_convert_fusion
  123.1 4.2 reshape.132
  127.3 6.0 reshape.105
  133.3 6.5 copy.18
  139.8 6.5 copy.25
  146.3 35.0 %while.31 = (s32[]{:T(128)}, f32[8,8,512]{2,1,0:T(8,128)S(1)}, bf16[8,500,512]{2,1,0:T(8,128)(2,1)}, bf16[8,500,250]{2,1,0:T(8,128)(2,1)}, bf16[8,250,512]{1,2,0:T(8,128)(2,1)}, /*index=5*/s32[]{:T(128)}) while((s32[]{:T(128)}, f32[8,8,512]{2,1,0:T(8,128)S(1)}, bf16[8,500,512]{2,1,0:T(8,128)(2,1)}, bf16[8,500,250]{2,1,0:T(8,128)(2,1)}, ...), condition=%wide.region_7.8_spmd, body=%wide.region_5.7_spmd.sunk | while | flops 1026171904 | bytes 4934221 | solution.py:33
  147.6 3.1 fusion.70
  152.0 3.1 fusion.70
  156.3 3.1 fusion.70
  160.7 3.1 fusion.70
  165.0 3.1 fusion.70
  169.4 3.1 fusion.70
  173.7 3.1 fusion.70
  178.1 3.1 fusion.70
  182.1 122.3 %all-reduce.6.cloned.1.call-done = f32[64,512]{1,0:T(8,128)} async-done(((f32[64,512]{1,0:T(8,128)}), f32[64,512]{1,0:T(8,128)}) %all-reduce.6.cloned.1.call-update) | async-done | bytes 131088
  305.2 863.1 %while.33 = (s32[]{:T(128)}, f32[8,512]{1,0:T(8,128)S(1)}, f32[2,512]{1,0:T(2,128)S(1)}, s32[]{:T(128)}, s32[]{:T(128)}, /*index=5*/f32[512,1024]{1,0:T(8,128)S(...) while((s32[]{:T(128)}, f32[8,512]{1,0:T(8,128)S(1)}, ...), condition=%wide.region_12.13_spmd.clone, body=%wide.region_9.12_spmd.clone.sunk | while | flops 41468964 | bytes 4176043 | solution.py:94
  305.6 10.0 while.34
  306.2 1.9 bitcast_dynamic-update-slice_fusion.5
  311.2 1.9 bitcast_dynamic-update-slice_fusion.5
  315.6 40.1 %custom-call.26 = f32[4,128,128]{1,2,0:T(8,128)S(1)} custom-call(f32[4,128,128]{2,1,0:T(8,128)} %get-tuple-element.386), custom_call_target="InvertDiagBlocksLowerTriangular" | custom-call | tf_op jit(solution)/shard_map/while/body/eval_jaxpr/jit(_solve_triangular)/triangular_solve | solution.py:83
  355.7 15.9 %psum.48 = f32[512,8]{0,1:T(8,128)S(1)} all-reduce(f32[512,8]{0,1:T(8,128)S(1)} %bitcast.105), channel_id=1, replica_groups=mesh['gen'=4,'fit'=8] {'gen'}, use_global_device_ids=true, to_apply=%region_10.10 | all-reduce | flops 4096 | bytes 32768 | tf_op jit(solution)/shard_map/while/body/eval_jaxpr/psum | solution.py:81
  373.1 38.4 %psum.49 = f32[8,512]{1,0:T(8,128)S(1)} all-reduce(f32[8,512]{1,0:T(8,128)S(1)} %fusion.88), channel_id=1, replica_groups=mesh['gen'=4,'fit'=8] {'gen','fit'}, use_global_device_ids=true, to_apply=%region_11.11 | all-reduce | flops 4096 | bytes 32768 | tf_op jit(solution)/shard_map/while/body/eval_jaxpr/psum | solution.py:12
  412.7 10.0 while.34
  413.4 1.9 bitcast_dynamic-update-slice_fusion.5
  418.4 1.9 bitcast_dynamic-update-slice_fusion.5
  422.8 40.1 %custom-call.26 = f32[4,128,128]{1,2,0:T(8,128)S(1)} custom-call(f32[4,128,128]{2,1,0:T(8,128)} %get-tuple-element.386), custom_call_target="InvertDiagBlocksLowerTriangular" | custom-call | tf_op jit(solution)/shard_map/while/body/eval_jaxpr/jit(_solve_triangular)/triangular_solve | solution.py:83
  462.9 16.7 %psum.48 = f32[512,8]{0,1:T(8,128)S(1)} all-reduce(f32[512,8]{0,1:T(8,128)S(1)} %bitcast.105), channel_id=1, replica_groups=mesh['gen'=4,'fit'=8] {'gen'}, use_global_device_ids=true, to_apply=%region_10.10 | all-reduce | flops 4096 | bytes 32768 | tf_op jit(solution)/shard_map/while/body/eval_jaxpr/psum | solution.py:81
  481.1 38.4 %psum.49 = f32[8,512]{1,0:T(8,128)S(1)} all-reduce(f32[8,512]{1,0:T(8,128)S(1)} %fusion.88), channel_id=1, replica_groups=mesh['gen'=4,'fit'=8] {'gen','fit'}, use_global_device_ids=true, to_apply=%region_11.11 | all-reduce | flops 4096 | bytes 32768 | tf_op jit(solution)/shard_map/while/body/eval_jaxpr/psum | solution.py:12
  520.7 10.0 while.34
  521.3 1.9 bitcast_dynamic-update-slice_fusion.5
  526.3 1.9 bitcast_dynamic-update-slice_fusion.5
  530.7 40.1 %custom-call.26 = f32[4,128,128]{1,2,0:T(8,128)S(1)} custom-call(f32[4,128,128]{2,1,0:T(8,128)} %get-tuple-element.386), custom_call_target="InvertDiagBlocksLowerTriangular" | custom-call | tf_op jit(solution)/shard_map/while/body/eval_jaxpr/jit(_solve_triangular)/triangular_solve | solution.py:83
  570.9 16.7 %psum.48 = f32[512,8]{0,1:T(8,128)S(1)} all-reduce(f32[512,8]{0,1:T(8,128)S(1)} %bitcast.105), channel_id=1, replica_groups=mesh['gen'=4,'fit'=8] {'gen'}, use_global_device_ids=true, to_apply=%region_10.10 | all-reduce | flops 4096 | bytes 32768 | tf_op jit(solution)/shard_map/while/body/eval_jaxpr/psum | solution.py:81
  589.1 38.4 %psum.49 = f32[8,512]{1,0:T(8,128)S(1)} all-reduce(f32[8,512]{1,0:T(8,128)S(1)} %fusion.88), channel_id=1, replica_groups=mesh['gen'=4,'fit'=8] {'gen','fit'}, use_global_device_ids=true, to_apply=%region_11.11 | all-reduce | flops 4096 | bytes 32768 | tf_op jit(solution)/shard_map/while/body/eval_jaxpr/psum | solution.py:12
  628.7 10.0 while.34
  629.3 1.9 bitcast_dynamic-update-slice_fusion.5
  638.7 40.1 %custom-call.26 = f32[4,128,128]{1,2,0:T(8,128)S(1)} custom-call(f32[4,128,128]{2,1,0:T(8,128)} %get-tuple-element.386), custom_call_target="InvertDiagBlocksLowerTriangular" | custom-call | tf_op jit(solution)/shard_map/while/body/eval_jaxpr/jit(_solve_triangular)/triangular_solve | solution.py:83
  678.8 16.7 %psum.48 = f32[512,8]{0,1:T(8,128)S(1)} all-reduce(f32[512,8]{0,1:T(8,128)S(1)} %bitcast.105), channel_id=1, replica_groups=mesh['gen'=4,'fit'=8] {'gen'}, use_global_device_ids=true, to_apply=%region_10.10 | all-reduce | flops 4096 | bytes 32768 | tf_op jit(solution)/shard_map/while/body/eval_jaxpr/psum | solution.py:81
  697.0 38.4 %psum.49 = f32[8,512]{1,0:T(8,128)S(1)} all-reduce(f32[8,512]{1,0:T(8,128)S(1)} %fusion.88), channel_id=1, replica_groups=mesh['gen'=4,'fit'=8] {'gen','fit'}, use_global_device_ids=true, to_apply=%region_11.11 | all-reduce | flops 4096 | bytes 32768 | tf_op jit(solution)/shard_map/while/body/eval_jaxpr/psum | solution.py:12
  736.6 10.0 while.34
  742.3 1.9 bitcast_dynamic-update-slice_fusion.5
  746.7 40.1 %custom-call.26 = f32[4,128,128]{1,2,0:T(8,128)S(1)} custom-call(f32[4,128,128]{2,1,0:T(8,128)} %get-tuple-element.386), custom_call_target="InvertDiagBlocksLowerTriangular" | custom-call | tf_op jit(solution)/shard_map/while/body/eval_jaxpr/jit(_solve_triangular)/triangular_solve | solution.py:83
  786.8 16.7 %psum.48 = f32[512,8]{0,1:T(8,128)S(1)} all-reduce(f32[512,8]{0,1:T(8,128)S(1)} %bitcast.105), channel_id=1, replica_groups=mesh['gen'=4,'fit'=8] {'gen'}, use_global_device_ids=true, to_apply=%region_10.10 | all-reduce | flops 4096 | bytes 32768 | tf_op jit(solution)/shard_map/while/body/eval_jaxpr/psum | solution.py:81
  805.0 38.4 %psum.49 = f32[8,512]{1,0:T(8,128)S(1)} all-reduce(f32[8,512]{1,0:T(8,128)S(1)} %fusion.88), channel_id=1, replica_groups=mesh['gen'=4,'fit'=8] {'gen','fit'}, use_global_device_ids=true, to_apply=%region_11.11 | all-reduce | flops 4096 | bytes 32768 | tf_op jit(solution)/shard_map/while/body/eval_jaxpr/psum | solution.py:12
  844.6 10.0 while.34
  845.2 1.9 bitcast_dynamic-update-slice_fusion.5
  854.6 40.1 %custom-call.26 = f32[4,128,128]{1,2,0:T(8,128)S(1)} custom-call(f32[4,128,128]{2,1,0:T(8,128)} %get-tuple-element.386), custom_call_target="InvertDiagBlocksLowerTriangular" | custom-call | tf_op jit(solution)/shard_map/while/body/eval_jaxpr/jit(_solve_triangular)/triangular_solve | solution.py:83
  894.8 16.8 %psum.48 = f32[512,8]{0,1:T(8,128)S(1)} all-reduce(f32[512,8]{0,1:T(8,128)S(1)} %bitcast.105), channel_id=1, replica_groups=mesh['gen'=4,'fit'=8] {'gen'}, use_global_device_ids=true, to_apply=%region_10.10 | all-reduce | flops 4096 | bytes 32768 | tf_op jit(solution)/shard_map/while/body/eval_jaxpr/psum | solution.py:81
  913.0 38.4 %psum.49 = f32[8,512]{1,0:T(8,128)S(1)} all-reduce(f32[8,512]{1,0:T(8,128)S(1)} %fusion.88), channel_id=1, replica_groups=mesh['gen'=4,'fit'=8] {'gen','fit'}, use_global_device_ids=true, to_apply=%region_11.11 | all-reduce | flops 4096 | bytes 32768 | tf_op jit(solution)/shard_map/while/body/eval_jaxpr/psum | solution.py:12
  952.5 10.0 while.34
  953.2 1.9 bitcast_dynamic-update-slice_fusion.5
  962.6 40.1 %custom-call.26 = f32[4,128,128]{1,2,0:T(8,128)S(1)} custom-call(f32[4,128,128]{2,1,0:T(8,128)} %get-tuple-element.386), custom_call_target="InvertDiagBlocksLowerTriangular" | custom-call | tf_op jit(solution)/shard_map/while/body/eval_jaxpr/jit(_solve_triangular)/triangular_solve | solution.py:83
  1002.7 16.8 %psum.48 = f32[512,8]{0,1:T(8,128)S(1)} all-reduce(f32[512,8]{0,1:T(8,128)S(1)} %bitcast.105), channel_id=1, replica_groups=mesh['gen'=4,'fit'=8] {'gen'}, use_global_device_ids=true, to_apply=%region_10.10 | all-reduce | flops 4096 | bytes 32768 | tf_op jit(solution)/shard_map/while/body/eval_jaxpr/psum | solution.py:81
  1020.9 38.4 %psum.49 = f32[8,512]{1,0:T(8,128)S(1)} all-reduce(f32[8,512]{1,0:T(8,128)S(1)} %fusion.88), channel_id=1, replica_groups=mesh['gen'=4,'fit'=8] {'gen','fit'}, use_global_device_ids=true, to_apply=%region_11.11 | all-reduce | flops 4096 | bytes 32768 | tf_op jit(solution)/shard_map/while/body/eval_jaxpr/psum | solution.py:12
  1060.5 10.0 while.34
  1070.6 40.1 %custom-call.26 = f32[4,128,128]{1,2,0:T(8,128)S(1)} custom-call(f32[4,128,128]{2,1,0:T(8,128)} %get-tuple-element.386), custom_call_target="InvertDiagBlocksLowerTriangular" | custom-call | tf_op jit(solution)/shard_map/while/body/eval_jaxpr/jit(_solve_triangular)/triangular_solve | solution.py:83
  1110.7 16.8 %psum.48 = f32[512,8]{0,1:T(8,128)S(1)} all-reduce(f32[512,8]{0,1:T(8,128)S(1)} %bitcast.105), channel_id=1, replica_groups=mesh['gen'=4,'fit'=8] {'gen'}, use_global_device_ids=true, to_apply=%region_10.10 | all-reduce | flops 4096 | bytes 32768 | tf_op jit(solution)/shard_map/while/body/eval_jaxpr/psum | solution.py:81
  1128.9 38.4 %psum.49 = f32[8,512]{1,0:T(8,128)S(1)} all-reduce(f32[8,512]{1,0:T(8,128)S(1)} %fusion.88), channel_id=1, replica_groups=mesh['gen'=4,'fit'=8] {'gen','fit'}, use_global_device_ids=true, to_apply=%region_11.11 | all-reduce | flops 4096 | bytes 32768 | tf_op jit(solution)/shard_map/while/body/eval_jaxpr/psum | solution.py:12
  (266 shorter events, 100.8 us)
Async XLA Ops:
  6.5 51.7 %all-gather.2.cloned.1.call-start = ((), (), s32[]{:S(2)}) async-start(), calls=%async_computation | async-start | bytes 4644864 | tf_op jit(solution)/shard_map/all_gather | solution.py:63
  7.3 139.0 %all-reduce.4.cloned.1.call-start = ((), (), s32[]{:S(2)}) async-start(), calls=%async_computation.1 | async-start | bytes 4194304 | tf_op jit(solution)/shard_map/psum | solution.py:12
  62.9 1.6 copy-start.1
  63.0 3.3 copy-start.3
  63.0 241.5 %all-reduce.6.cloned.1.call-start = ((), (), s32[]{:S(2)}) async-start(), calls=%async_computation.2 | async-start | bytes 262144
  146.3 158.9 %copy-start = (f32[512,1024]{1,0:T(8,128)S(1)}, f32[512,1024]{1,0:T(8,128)}, u32[]{:S(2)}) copy-start(f32[512,1024]{1,0:T(8,128)} %param.11) | copy-start | bytes 6291460
  1168.3 0.6 copy-start.2
Sparse Core Ops, SparseCore 0:
  9.0 49.1 all-gather.1
  63.1 69.2 all-reduce.3
  182.2 122.1 all-reduce.5
where the time goes:
time: 1180 us
  blocking collectives  480 us (41%)
  other arithmetic  328 us (28%)
  waiting for transfers between devices  174 us (15%)
  local copies, waits for them, and re-layouts  132 us (11%)
  matrix products  47.8 us (4%)
  between operations  13.3 us (1%)
    another operation x24, other arithmetic, advance(): jax.scipy.linalg.solve_triangular(column_part, whole_rest.T, lower=True)  322 us
    psum x8, blocking collectives, spread(): return lax.psum(kept, axis)  307 us
    psum x8, blocking collectives, advance(): whole_rest = lax.psum(remaining, 'gen')  133 us
    unnamed x4, waiting for transfers between devices  123 us
    another operation x96, local copies, waits for them, and re-layouts  80.2 us
    all_gather x1, waiting for transfers between devices, on_device(): orbital_side = lax.all_gather(collocation, 'fit', axis=1, tiled=True)  50.9 us
    psum x1, blocking collectives, on_device(): pivot_block = lax.psum(own_entries, ('gen', 'fit'))  39.1 us
    dot_general x8, matrix products, one_block(): jnp.einsum('apq,pn->aqn', vectors, pieces[0], preferred_element_type=jnp....  25.1 us
  transfers between devices with their start and end apart: 3, of which 2 were waited for; matrix products, arithmetic and copies ran while one was open for 4% of the time, Pallas kernels for 0%

commit v1 on v0

--- a/solution.py
+++ b/solution.py
@@ -60,7 +60,14 @@
     group_ratio = fit_count // gen_count
     owner_index = fit_index // group_ratio
     portion = fit_index % group_ratio
-    orbital_side = lax.all_gather(collocation, "fit", axis=1, tiled=True)
+    size = lax.axis_size("fit")
+    right = [(i, (i + 1) % size) for i in range(size)]
+    parts = [collocation]
+    for far in range(1, size):
+        parts = [lax.ppermute(parts[0], "fit", right), *parts]
+    whole = jnp.concatenate(parts, axis=1)
+    offset = (lax.axis_index("fit") + 1) * parts[-1].shape[1]
+    orbital_side = jnp.roll(whole, offset, axis=1)
     wide_slice = lax.dynamic_slice_in_dim(orbital_side, portion * pair_block, pair_block, 0)
     pair_side = spread(wide_slice, "gen", owner_index)
     partial_panel = project_block(

time: 1180 us -> 1210 us (1.025)
  waiting for transfers between devices: 174 us -> 196 us
    ppermute x0 -> x7, waiting for transfers between devices: none -> 72.7 us  [on_device(): parts = [lax.ppermute(parts[0], 'fit', right), *parts]]
    all_gather x1 -> x0, waiting for transfers between devices: 50.9 us -> none  [on_device(): orbital_side = lax.all_gather(collocation, 'fit', axis=1, tiled=True)]
    unnamed x4 -> x3, waiting for transfers between devices: 123 us -> 123 us
  transfers between devices with their start and end apart: 3 -> 9, of which waited for: 2 -> 8; matrix products, arithmetic and copies ran while one was open for 4% -> 4% of each run, Pallas kernels for 0% -> 0%
where the time goes in v1:
time: 1210 us
  blocking collectives  479 us (40%)
  other arithmetic  327 us (27%)
  waiting for transfers between devices  196 us (16%)
  local copies, waits for them, and re-layouts  143 us (12%)
  matrix products  49.3 us (4%)
  between operations  13.7 us (1%)
    another operation x24, other arithmetic, advance(): jax.scipy.linalg.solve_triangular(column_part, whole_rest.T, lower=True)  322 us
    psum x8, blocking collectives, spread(): return lax.psum(kept, axis)  307 us
    psum x8, blocking collectives, advance(): whole_rest = lax.psum(remaining, 'gen')  133 us
    unnamed x3, waiting for transfers between devices  123 us
    another operation x96, local copies, waits for them, and re-layouts  80.2 us
    ppermute x7, waiting for transfers between devices, on_device(): parts = [lax.ppermute(parts[0], 'fit', right), *parts]  72.7 us
    psum x1, blocking collectives, on_device(): pivot_block = lax.psum(own_entries, ('gen', 'fit'))  38.6 us
    dot_general x8, matrix products, one_block(): jnp.einsum('apq,pn->aqn', vectors, pieces[0], preferred_element_type=jnp....  25.1 us
  transfers between devices with their start and end apart: 9, of which 8 were waited for; matrix products, arithmetic and copies ran while one was open for 4% of the time, Pallas kernels for 0%

profile of v1, /device:TPU:0, one launch (start us, length us, event | category | flops | bytes accessed | tf_op | source)
XLA Modules:
  0.0 1210.1 jit_solution(4453519686493123997)
XLA Ops:
  7.0 11.1 collective-permute-done
  18.1 10.3 collective-permute-done.1
  28.4 10.3 collective-permute-done.2
  38.7 10.3 collective-permute-done.3
  49.0 10.3 collective-permute-done.4
  59.4 10.4 collective-permute-done.5
  70.4 10.0 collective-permute-done.6
  86.6 3.2 copy-done.1
  90.8 2.5 copy.24
  93.4 2.0 copy.19
  95.5 2.1 fusion.28
  97.7 38.6 %psum.42 = f32[8,8]{0,1:T(8,128)S(1)} all-reduce(f32[8,8]{0,1:T(8,128)S(1)} %bitcast.108), channel_id=1, replica_groups=mesh['gen'=4,'fit'=8] {'gen','fit'}, use_global_device_ids=true, to_apply=%region_2.3 | all-reduce | flops 64 | bytes 512 | tf_op jit(solution)/shard_map/psum | solution.py:55
  139.1 5.8 reshape.130
  144.9 4.0 reshape.104
  148.9 3.0 convolution_convert_fusion
  151.9 4.2 reshape.132
  156.1 6.0 reshape.105
  162.1 4.6 constant_dynamic-slice_fusion.2
  166.7 6.5 copy.18
  173.2 6.5 copy.25
  179.7 35.0 %while.31 = (s32[]{:T(128)}, f32[8,8,512]{2,1,0:T(8,128)S(1)}, bf16[8,500,512]{2,1,0:T(8,128)(2,1)}, bf16[8,500,250]{2,1,0:T(8,128)(2,1)}, bf16[8,250,512]{1,2,0:T(8,128)(2,1)}, /*index=5*/s32[]{:T(128)}) while((s32[]{:T(128)}, f32[8,8,512]{2,1,0:T(8,128)S(1)}, bf16[8,500,512]{2,1,0:T(8,128)(2,1)}, bf16[8,500,250]{2,1,0:T(8,128)(2,1)}, ...), condition=%wide.region_7.8_spmd, body=%wide.region_5.7_spmd.sunk | while | flops 1026171904 | bytes 4934221 | solution.py:33
  181.0 3.1 fusion.70
  185.4 3.1 fusion.70
  189.7 3.1 fusion.70
  194.1 3.1 fusion.70
  198.4 3.1 fusion.70
  202.8 3.1 fusion.70
  207.2 3.1 fusion.70
  211.5 3.1 fusion.70
  215.6 123.2 %all-reduce.6.cloned.1.call-done = f32[64,512]{1,0:T(8,128)} async-done(((f32[64,512]{1,0:T(8,128)}), f32[64,512]{1,0:T(8,128)}) %all-reduce.6.cloned.1.call-update) | async-done | bytes 131088
  339.5 863.1 %while.33 = (s32[]{:T(128)}, f32[8,512]{1,0:T(8,128)S(1)}, f32[2,512]{1,0:T(2,128)S(1)}, s32[]{:T(128)}, s32[]{:T(128)}, /*index=5*/f32[512,1024]{1,0:T(8,128)S(...) while((s32[]{:T(128)}, f32[8,512]{1,0:T(8,128)S(1)}, ...), condition=%wide.region_12.13_spmd.clone, body=%wide.region_9.12_spmd.clone.sunk | while | flops 41468964 | bytes 4176043 | solution.py:101
  340.0 10.0 while.34
  350.0 40.1 %custom-call.28 = f32[4,128,128]{1,2,0:T(8,128)S(1)} custom-call(f32[4,128,128]{2,1,0:T(8,128)} %get-tuple-element.386), custom_call_target="InvertDiagBlocksLowerTriangular" | custom-call | tf_op jit(solution)/shard_map/while/body/eval_jaxpr/jit(_solve_triangular)/triangular_solve | solution.py:90
  390.1 15.9 %psum.48 = f32[512,8]{0,1:T(8,128)S(1)} all-reduce(f32[512,8]{0,1:T(8,128)S(1)} %bitcast.105), channel_id=1, replica_groups=mesh['gen'=4,'fit'=8] {'gen'}, use_global_device_ids=true, to_apply=%region_10.10 | all-reduce | flops 4096 | bytes 32768 | tf_op jit(solution)/shard_map/while/body/eval_jaxpr/psum | solution.py:88
  407.5 38.4 %psum.49 = f32[8,512]{1,0:T(8,128)S(1)} all-reduce(f32[8,512]{1,0:T(8,128)S(1)} %fusion.88), channel_id=1, replica_groups=mesh['gen'=4,'fit'=8] {'gen','fit'}, use_global_device_ids=true, to_apply=%region_11.11 | all-reduce | flops 4096 | bytes 32768 | tf_op jit(solution)/shard_map/while/body/eval_jaxpr/psum | solution.py:12
  447.1 10.0 while.34
  457.2 40.1 %custom-call.28 = f32[4,128,128]{1,2,0:T(8,128)S(1)} custom-call(f32[4,128,128]{2,1,0:T(8,128)} %get-tuple-element.386), custom_call_target="InvertDiagBlocksLowerTriangular" | custom-call | tf_op jit(solution)/shard_map/while/body/eval_jaxpr/jit(_solve_triangular)/triangular_solve | solution.py:90
  497.3 16.7 %psum.48 = f32[512,8]{0,1:T(8,128)S(1)} all-reduce(f32[512,8]{0,1:T(8,128)S(1)} %bitcast.105), channel_id=1, replica_groups=mesh['gen'=4,'fit'=8] {'gen'}, use_global_device_ids=true, to_apply=%region_10.10 | all-reduce | flops 4096 | bytes 32768 | tf_op jit(solution)/shard_map/while/body/eval_jaxpr/psum | solution.py:88
  515.5 38.4 %psum.49 = f32[8,512]{1,0:T(8,128)S(1)} all-reduce(f32[8,512]{1,0:T(8,128)S(1)} %fusion.88), channel_id=1, replica_groups=mesh['gen'=4,'fit'=8] {'gen','fit'}, use_global_device_ids=true, to_apply=%region_11.11 | all-reduce | flops 4096 | bytes 32768 | tf_op jit(solution)/shard_map/while/body/eval_jaxpr/psum | solution.py:12
  555.1 10.0 while.34
  555.7 1.9 bitcast_dynamic-update-slice_fusion.5
  565.1 40.1 %custom-call.28 = f32[4,128,128]{1,2,0:T(8,128)S(1)} custom-call(f32[4,128,128]{2,1,0:T(8,128)} %get-tuple-element.386), custom_call_target="InvertDiagBlocksLowerTriangular" | custom-call | tf_op jit(solution)/shard_map/while/body/eval_jaxpr/jit(_solve_triangular)/triangular_solve | solution.py:90
  605.2 16.7 %psum.48 = f32[512,8]{0,1:T(8,128)S(1)} all-reduce(f32[512,8]{0,1:T(8,128)S(1)} %bitcast.105), channel_id=1, replica_groups=mesh['gen'=4,'fit'=8] {'gen'}, use_global_device_ids=true, to_apply=%region_10.10 | all-reduce | flops 4096 | bytes 32768 | tf_op jit(solution)/shard_map/while/body/eval_jaxpr/psum | solution.py:88
  623.4 38.4 %psum.49 = f32[8,512]{1,0:T(8,128)S(1)} all-reduce(f32[8,512]{1,0:T(8,128)S(1)} %fusion.88), channel_id=1, replica_groups=mesh['gen'=4,'fit'=8] {'gen','fit'}, use_global_device_ids=true, to_apply=%region_11.11 | all-reduce | flops 4096 | bytes 32768 | tf_op jit(solution)/shard_map/while/body/eval_jaxpr/psum | solution.py:12
  663.0 10.0 while.34
  673.1 40.1 %custom-call.28 = f32[4,128,128]{1,2,0:T(8,128)S(1)} custom-call(f32[4,128,128]{2,1,0:T(8,128)} %get-tuple-element.386), custom_call_target="InvertDiagBlocksLowerTriangular" | custom-call | tf_op jit(solution)/shard_map/while/body/eval_jaxpr/jit(_solve_triangular)/triangular_solve | solution.py:90
  713.2 16.7 %psum.48 = f32[512,8]{0,1:T(8,128)S(1)} all-reduce(f32[512,8]{0,1:T(8,128)S(1)} %bitcast.105), channel_id=1, replica_groups=mesh['gen'=4,'fit'=8] {'gen'}, use_global_device_ids=true, to_apply=%region_10.10 | all-reduce | flops 4096 | bytes 32768 | tf_op jit(solution)/shard_map/while/body/eval_jaxpr/psum | solution.py:88
  731.4 38.4 %psum.49 = f32[8,512]{1,0:T(8,128)S(1)} all-reduce(f32[8,512]{1,0:T(8,128)S(1)} %fusion.88), channel_id=1, replica_groups=mesh['gen'=4,'fit'=8] {'gen','fit'}, use_global_device_ids=true, to_apply=%region_11.11 | all-reduce | flops 4096 | bytes 32768 | tf_op jit(solution)/shard_map/while/body/eval_jaxpr/psum | solution.py:12
  771.0 10.0 while.34
  781.0 40.1 %custom-call.28 = f32[4,128,128]{1,2,0:T(8,128)S(1)} custom-call(f32[4,128,128]{2,1,0:T(8,128)} %get-tuple-element.386), custom_call_target="InvertDiagBlocksLowerTriangular" | custom-call | tf_op jit(solution)/shard_map/while/body/eval_jaxpr/jit(_solve_triangular)/triangular_solve | solution.py:90
  821.2 16.7 %psum.48 = f32[512,8]{0,1:T(8,128)S(1)} all-reduce(f32[512,8]{0,1:T(8,128)S(1)} %bitcast.105), channel_id=1, replica_groups=mesh['gen'=4,'fit'=8] {'gen'}, use_global_device_ids=true, to_apply=%region_10.10 | all-reduce | flops 4096 | bytes 32768 | tf_op jit(solution)/shard_map/while/body/eval_jaxpr/psum | solution.py:88
  839.4 38.4 %psum.49 = f32[8,512]{1,0:T(8,128)S(1)} all-reduce(f32[8,512]{1,0:T(8,128)S(1)} %fusion.88), channel_id=1, replica_groups=mesh['gen'=4,'fit'=8] {'gen','fit'}, use_global_device_ids=true, to_apply=%region_11.11 | all-reduce | flops 4096 | bytes 32768 | tf_op jit(solution)/shard_map/while/body/eval_jaxpr/psum | solution.py:12
  878.9 10.0 while.34
  889.0 40.1 %custom-call.28 = f32[4,128,128]{1,2,0:T(8,128)S(1)} custom-call(f32[4,128,128]{2,1,0:T(8,128)} %get-tuple-element.386), custom_call_target="InvertDiagBlocksLowerTriangular" | custom-call | tf_op jit(solution)/shard_map/while/body/eval_jaxpr/jit(_solve_triangular)/triangular_solve | solution.py:90
  929.1 16.8 %psum.48 = f32[512,8]{0,1:T(8,128)S(1)} all-reduce(f32[512,8]{0,1:T(8,128)S(1)} %bitcast.105), channel_id=1, replica_groups=mesh['gen'=4,'fit'=8] {'gen'}, use_global_device_ids=true, to_apply=%region_10.10 | all-reduce | flops 4096 | bytes 32768 | tf_op jit(solution)/shard_map/while/body/eval_jaxpr/psum | solution.py:88
  947.3 38.4 %psum.49 = f32[8,512]{1,0:T(8,128)S(1)} all-reduce(f32[8,512]{1,0:T(8,128)S(1)} %fusion.88), channel_id=1, replica_groups=mesh['gen'=4,'fit'=8] {'gen','fit'}, use_global_device_ids=true, to_apply=%region_11.11 | all-reduce | flops 4096 | bytes 32768 | tf_op jit(solution)/shard_map/while/body/eval_jaxpr/psum | solution.py:12
  986.9 10.0 while.34
  996.9 40.1 %custom-call.28 = f32[4,128,128]{1,2,0:T(8,128)S(1)} custom-call(f32[4,128,128]{2,1,0:T(8,128)} %get-tuple-element.386), custom_call_target="InvertDiagBlocksLowerTriangular" | custom-call | tf_op jit(solution)/shard_map/while/body/eval_jaxpr/jit(_solve_triangular)/triangular_solve | solution.py:90
  1037.1 16.8 %psum.48 = f32[512,8]{0,1:T(8,128)S(1)} all-reduce(f32[512,8]{0,1:T(8,128)S(1)} %bitcast.105), channel_id=1, replica_groups=mesh['gen'=4,'fit'=8] {'gen'}, use_global_device_ids=true, to_apply=%region_10.10 | all-reduce | flops 4096 | bytes 32768 | tf_op jit(solution)/shard_map/while/body/eval_jaxpr/psum | solution.py:88
  1055.3 38.4 %psum.49 = f32[8,512]{1,0:T(8,128)S(1)} all-reduce(f32[8,512]{1,0:T(8,128)S(1)} %fusion.88), channel_id=1, replica_groups=mesh['gen'=4,'fit'=8] {'gen','fit'}, use_global_device_ids=true, to_apply=%region_11.11 | all-reduce | flops 4096 | bytes 32768 | tf_op jit(solution)/shard_map/while/body/eval_jaxpr/psum | solution.py:12
  1094.8 10.0 while.34
  1104.9 40.1 %custom-call.28 = f32[4,128,128]{1,2,0:T(8,128)S(1)} custom-call(f32[4,128,128]{2,1,0:T(8,128)} %get-tuple-element.386), custom_call_target="InvertDiagBlocksLowerTriangular" | custom-call | tf_op jit(solution)/shard_map/while/body/eval_jaxpr/jit(_solve_triangular)/triangular_solve | solution.py:90
  1145.0 16.8 %psum.48 = f32[512,8]{0,1:T(8,128)S(1)} all-reduce(f32[512,8]{0,1:T(8,128)S(1)} %bitcast.105), channel_id=1, replica_groups=mesh['gen'=4,'fit'=8] {'gen'}, use_global_device_ids=true, to_apply=%region_10.10 | all-reduce | flops 4096 | bytes 32768 | tf_op jit(solution)/shard_map/while/body/eval_jaxpr/psum | solution.py:88
  1163.2 38.4 %psum.49 = f32[8,512]{1,0:T(8,128)S(1)} all-reduce(f32[8,512]{1,0:T(8,128)S(1)} %fusion.88), channel_id=1, replica_groups=mesh['gen'=4,'fit'=8] {'gen','fit'}, use_global_device_ids=true, to_apply=%region_11.11 | all-reduce | flops 4096 | bytes 32768 | tf_op jit(solution)/shard_map/while/body/eval_jaxpr/psum | solution.py:12
  (294 shorter events, 121.7 us)
Async XLA Ops:
  6.5 80.0 %copy-start.2 = (bf16[500,512]{1,0:T(8,128)(2,1)S(1)}, bf16[500,512]{1,0:T(8,128)(2,1)}, u32[]{:S(2)}) copy-start(bf16[500,512]{1,0:T(8,128)(2,1)} %param.10) | copy-start | bytes 1536004
  6.5 173.2 %all-reduce.4.cloned.1.call-start = ((), (), s32[]{:S(2)}) async-start(), calls=%async_computation | async-start | bytes 4194304 | tf_op jit(solution)/shard_map/psum | solution.py:12
  6.5 11.5 collective-permute-start
  18.1 10.3 collective-permute-start.1
  28.4 10.3 collective-permute-start.2
  38.7 10.3 collective-permute-start.3
  49.0 10.3 collective-permute-start.4
  59.4 10.4 collective-permute-start.5
  69.8 10.6 collective-permute-start.6
  86.6 3.2 copy-start.1
  93.4 245.4 %all-reduce.6.cloned.1.call-start = ((), (), s32[]{:S(2)}) async-start(), calls=%async_computation.1 | async-start | bytes 262144
  179.7 159.8 %copy-start = (f32[512,1024]{1,0:T(8,128)S(1)}, f32[512,1024]{1,0:T(8,128)}, u32[]{:S(2)}) copy-start(f32[512,1024]{1,0:T(8,128)} %param.11) | copy-start | bytes 6291460
  1202.6 0.6 copy-start.3
Sparse Core Ops, SparseCore 0:
  93.5 68.9 all-reduce.3
  215.7 123.0 all-reduce.5
